TPU v7x, 32 devices: a whole 2x2x4 slice. The times are simulated.
32 devices in a mesh: pb: 8 (over z, y), ka: 2 (over x), ha: 2 (over core).
Axes of the slice: x: 2, y: 2, z: 4, core: 2. Of those that a mesh axis runs over, the one named last changes fastest.
Arguments:
- queries: bfloat16 [8192, 256], P(('pb', 'ka'), 'ha'), may hold values from -130 to 130
- key_codes: int32 [8192, 256], P(('ka', 'pb'), 'ha'), may hold values from -127 to 127
- value_codes: int32 [8192, 256], P(('ka', 'pb'), 'ha'), may hold values from -127 to 127
- key_scale: float32 [], replicated, may hold values from 0.015 to 0.02
- value_scale: float32 [], replicated, may hold values from 0.01 to 0.02
- out_grad: bfloat16 [8192, 256], P(('pb', 'ka'), 'ha'), may hold values from -256 to 256
Outputs:
- query_grad: float32 [8192, 256], P(('pb', 'ka'), 'ha')
- key_grad: float32 [8192, 256], P(('ka', 'pb'), 'ha')
- value_grad: float32 [8192, 256], P(('ka', 'pb'), 'ha')
All inputs are finite; a program needn't handle non-finite values.
Results may differ from a plain program's by a relative error of at most 0.017.
Values may be sent and summed in bfloat16 or wider, within the bound.
A program may use at most 128 MiB of HBM per device.

v0:
```python
import math
import jax
import jax.numpy as jnp
from jax import lax
from jax.sharding import PartitionSpec as P


def merged(part, axis, combine):
    gathered = jax.tree.map(lambda a: lax.all_gather(a, axis), part)

    def take(source):
        return jax.tree.map(lambda a: lax.dynamic_index_in_dim(a, source, 0, False), gathered)

    return lax.fori_loop(
        1, lax.axis_size(axis), lambda source, state: combine(state, take(source)), take(0)
    )


def dequantize(table, factor):
    return (table.astype(jnp.float32) * factor).astype(jnp.bfloat16)


def contract_last(left, right):
    return lax.dot_general(
        left, right, (((1,), (1,)), ((), ())), preferred_element_type=jnp.float32
    )


def contract_first(left, right):
    return lax.dot_general(
        left, right, (((0,), (0,)), ((), ())), preferred_element_type=jnp.float32
    )


def merge_two(first, second):
    max_a, sum_a = first
    max_b, sum_b = second
    top = jnp.maximum(max_a, max_b)
    return (top, sum_a * jnp.exp(max_a - top) + sum_b * jnp.exp(max_b - top))


def shards(queries, key_codes, value_codes, key_scale, value_scale, out_grad):
    width = queries.shape[1]
    factor = 1.0 / math.sqrt(width)
    q_full, d_full = (
        lax.all_gather(queries, "ka", axis=0, tiled=True),
        lax.all_gather(out_grad, "ka", axis=0, tiled=True),
    )
    key_rows, value_rows = (
        lax.all_gather(key_codes.astype(jnp.bfloat16), "pb", axis=0, tiled=True),
        lax.all_gather(value_codes.astype(jnp.bfloat16), "pb", axis=0, tiled=True),
    )
    keys = dequantize(key_rows, key_scale)
    values = dequantize(value_rows, value_scale)
    rows = q_full.shape[0]
    block_rows = 512
    block_count = rows // block_rows
    q_blocks = q_full.reshape(block_count, block_rows, width)
    d_blocks = d_full.reshape(block_count, block_rows, width)

    def first_pass(totals, inputs):
        q_block, d_block = inputs
        scores = contract_last(q_block, keys) * factor
        row_max = jnp.max(scores, axis=1)
        shifted = jnp.exp(scores - row_max[:, None])
        d_probs = contract_last(d_block, values)
        return (
            totals,
            (
                row_max,
                jnp.sum(shifted, axis=1),
                jnp.sum(shifted * d_probs, axis=1),
                scores,
                d_probs,
            ),
        )

    _, (row_max, row_sum, row_dot, score_tiles, dprob_tiles) = lax.scan(
        first_pass, jnp.float32(0.0), (q_blocks, d_blocks)
    )
    row_max = row_max.reshape(rows)
    row_sum = row_sum.reshape(rows)
    row_dot = row_dot.reshape(rows)
    full_max, full_sum = merged((row_max, row_sum), "ka", merge_two)
    log_total = full_max + jnp.log(full_sum)
    delta_rows = lax.psum(row_dot * jnp.exp(row_max - log_total), "ka")
    lse_blocks = log_total.reshape(block_count, block_rows)
    delta_blocks = delta_rows.reshape(block_count, block_rows)

    def tile_terms(scores, d_probs, lse_block, delta_block):
        probs = jnp.exp(scores - lse_block[:, None])
        d_scores = probs * (d_probs - delta_block[:, None])
        return (probs.astype(jnp.bfloat16), d_scores.astype(jnp.bfloat16))

    def second_full(totals, inputs):
        k_grad, v_grad = totals
        q_block, d_block, scores, d_probs, lse_block, delta_block = inputs
        probs_low, d_scores_low = tile_terms(scores, d_probs, lse_block, delta_block)
        q_grad = jnp.dot(d_scores_low, keys, preferred_element_type=jnp.float32) * factor
        k_grad = k_grad + contract_first(d_scores_low, q_block) * factor
        v_grad = v_grad + contract_first(probs_low, d_block)
        return ((k_grad, v_grad), q_grad)

    inputs = (q_blocks, d_blocks, score_tiles, dprob_tiles, lse_blocks, delta_blocks)
    zeros = jnp.zeros((keys.shape[0], width), jnp.float32)
    (k_grad, v_grad), q_grad = lax.scan(second_full, (zeros, zeros), inputs)
    stacked = jnp.concatenate([k_grad, v_grad], axis=1)
    summed = lax.psum_scatter(
        stacked.astype(jnp.bfloat16), "pb", scatter_dimension=0, tiled=True
    ).astype(jnp.float32)
    key_grad = summed[:, :width]
    value_grad = summed[:, width:]
    query_grad = lax.psum_scatter(
        q_grad.reshape(rows, width).astype(jnp.bfloat16), "ka", scatter_dimension=0, tiled=True
    ).astype(jnp.float32)
    return (query_grad, key_grad, value_grad)


def solution(mesh):
    in_specs = (
        P(("pb", "ka"), "ha"),
        P(("ka", "pb"), "ha"),
        P(("ka", "pb"), "ha"),
        P(),
        P(),
        P(("pb", "ka"), "ha"),
    )
    out_specs = (P(("pb", "ka"), "ha"), P(("ka", "pb"), "ha"), P(("ka", "pb"), "ha"))
    return jax.shard_map(shards, mesh=mesh, in_specs=in_specs, out_specs=out_specs, check_vma=False)
```

profile of v0, /device:TPU:0, one launch (start us, length us, event | category | flops | bytes accessed | tf_op | source)
XLA Modules:
  0.0 266.3 jit_solution(2322853706921836254)
XLA Ops:
  7.2 1.6 convert_element_type.45
  8.9 1.6 convert_element_type.48
  12.0 7.4 %all_gather.18 = bf16[1024,128]{1,0:T(8,128)(2,1)S(1)} all-gather(bf16[512,128]{1,0:T(8,128)(2,1)} %param.10), channel_id=1, replica_groups=mesh['pb'=8,'ka'=2,'ha'=2] {'ka'}, dimensions={0}, use_global_device_ids=true | all-gather | bytes 393216 | tf_op jit(solution)/shard_map/all_gather | solution.py:46
  19.3 7.2 %all_gather.20 = bf16[1024,128]{1,0:T(8,128)(2,1)} all-gather(bf16[512,128]{1,0:T(8,128)(2,1)} %param.15), channel_id=1, replica_groups=mesh['pb'=8,'ka'=2,'ha'=2] {'ka'}, dimensions={0}, use_global_device_ids=true | all-gather | bytes 393216 | tf_op jit(solution)/shard_map/all_gather | solution.py:47
  26.5 27.2 %all-gather.5.cloned.1.call-done = bf16[4096,128]{1,0:T(8,128)(2,1)} async-done(((bf16[512,128]{1,0:T(8,128)(2,1)}), bf16[4096,128]{1,0:T(8,128)(2,1)}) %all-gather.5.cloned.1.call-update) | async-done | bytes 1048592 | tf_op jit(solution)/shard_map/all_gather | solution.py:50
  53.6 1.4 multiply_convert_fusion.2
  55.1 40.2 %all-gather.7.cloned.1.call-done = bf16[4096,128]{1,0:T(8,128)(2,1)} async-done(((bf16[512,128]{1,0:T(8,128)(2,1)}), bf16[4096,128]{1,0:T(8,128)(2,1)}) %all-gather.7.cloned.1.call-update) | async-done | bytes 1048592 | tf_op jit(solution)/shard_map/all_gather | solution.py:51
  95.3 2.4 multiply_convert_fusion.1
  97.7 21.8 %while.13 = (s32[]{:T(128)}, f32[2,512]{1,0:T(2,128)S(1)}, f32[2,512]{1,0:T(2,128)S(1)}, f32[2,512]{1,0:T(2,128)S(1)}, f32[2,512,4096]{2,1,0:T(8,128)}, /*index=...) while((s32[]{:T(128)}, f32[2,512]{1,0:T(2,128)S(1)}, ...), condition=%wide.region_4.5_spmd, body=%wide.region_0.4_spmd.sunk | while | flops 1090517504 | bytes 66343616 | solution.py:78
  97.7 1.3 multiply_reduce_fusion.4
  99.0 3.0 %multiply_reduce_fusion.5 = (f32[512]{0:T(512)S(1)}, f32[512]{0:T(512)S(1)}, f32[512,4096]{1,0:T(8,128)S(1)}) fusion(f32[512,4096]{1,0:T(8,128)S(1)} %get-tuple-element.372, f32[512]{0:T(512)S(1)} %get-tuple-element.371, bf16[4096,128]{1,0:T(8,128)(2,1)S(1)} %copy-done.1, bf16[2,512,128]{2,1,0:T(8,128)(2,1)S(1)} %copy-done.2, s32[]{:T(128)} %get-tuple-element.403), kind=kOutput, calls=%fused_computation.2.clone.1 | convolution fusion | flops 547355648 | bytes 17963012 | tf_op jit(solution)/shard_map/while/body/eval_jaxpr/dot_general | solution.py:24
  102.0 6.4 %bitcast_dynamic-update-slice_fusion.3 = (f32[2,512,4096]{2,1,0:T(8,128)}, f32[2,512,4096]{2,1,0:T(8,128)}) fusion(f32[2,512,4096]{2,1,0:T(8,128)} %get-tuple-element.408, s32[]{:T(128)} %get-tuple-element.403, f32[512,4096]{1,0:T(8,128)S(1)} %get-tuple-element.375, f32[2,512,4096]{2,1,0:T(8,128)} %get-tuple-element.407, ...), kind=kLoop, calls=%fused_computation.clone.1 | loop fusion | flops 2097152 | bytes 33554944 | tf_op jit(solution)/shard_map/while/body/jit(dynamic_update_index_in_dim)/dynamic_update_slice | solution.py:78
  108.6 1.3 multiply_reduce_fusion.4
  109.9 3.0 %multiply_reduce_fusion.5 = (f32[512]{0:T(512)S(1)}, f32[512]{0:T(512)S(1)}, f32[512,4096]{1,0:T(8,128)S(1)}) fusion(f32[512,4096]{1,0:T(8,128)S(1)} %get-tuple-element.372, f32[512]{0:T(512)S(1)} %get-tuple-element.371, bf16[4096,128]{1,0:T(8,128)(2,1)S(1)} %copy-done.1, bf16[2,512,128]{2,1,0:T(8,128)(2,1)S(1)} %copy-done.2, s32[]{:T(128)} %get-tuple-element.403), kind=kOutput, calls=%fused_computation.2.clone.1 | convolution fusion | flops 547355648 | bytes 17963012 | tf_op jit(solution)/shard_map/while/body/eval_jaxpr/dot_general | solution.py:24
  112.9 6.4 %bitcast_dynamic-update-slice_fusion.3 = (f32[2,512,4096]{2,1,0:T(8,128)}, f32[2,512,4096]{2,1,0:T(8,128)}) fusion(f32[2,512,4096]{2,1,0:T(8,128)} %get-tuple-element.408, s32[]{:T(128)} %get-tuple-element.403, f32[512,4096]{1,0:T(8,128)S(1)} %get-tuple-element.375, f32[2,512,4096]{2,1,0:T(8,128)} %get-tuple-element.407, ...), kind=kLoop, calls=%fused_computation.clone.1 | loop fusion | flops 2097152 | bytes 33554944 | tf_op jit(solution)/shard_map/while/body/jit(dynamic_update_index_in_dim)/dynamic_update_slice | solution.py:78
  119.5 4.3 %all-gather = f32[2,1,1024]{2,1,0:T(1,128)S(1)} all-gather(f32[1,1,1024]{2,1,0:T(1,128)S(1)} %reshape.58), channel_id=1, replica_groups=mesh['pb'=8,'ka'=2,'ha'=2] {'ka'}, dimensions={0}, use_global_device_ids=true | all-gather | bytes 12288 | tf_op jit(solution)/shard_map/all_gather | solution.py:9
  123.8 4.3 %all-gather.1 = f32[2,1,1024]{2,1,0:T(1,128)S(1)} all-gather(f32[1,1,1024]{2,1,0:T(1,128)S(1)} %reshape.60), channel_id=1, replica_groups=mesh['pb'=8,'ka'=2,'ha'=2] {'ka'}, dimensions={0}, use_global_device_ids=true | all-gather | bytes 12288 | tf_op jit(solution)/shard_map/all_gather | solution.py:9
  128.2 4.9 %psum.7 = f32[2,512]{1,0:T(2,128)S(1)} all-reduce(f32[2,512]{1,0:T(2,128)S(1)} %reshape.57), channel_id=1, replica_groups=mesh['pb'=8,'ka'=2,'ha'=2] {'ka'}, use_global_device_ids=true, to_apply=%region_5.6 | all-reduce | flops 1024 | bytes 8192 | tf_op jit(solution)/shard_map/psum | solution.py:86
  133.3 42.3 %while.40 = (s32[]{:T(128)}, f32[4096,128]{1,0:T(8,128)S(1)}, f32[4096,128]{1,0:T(8,128)}, bf16[2,512,128]{2,1,0:T(8,128)(2,1)}, f32[2,512,4096]{2,1,0:T(8,128)}...) while((s32[]{:T(128)}, f32[4096,128]{1,0:T(8,128)S(1)}, ...), condition=%wide.region_7.8_spmd.clone, body=%wide.region_6.7_spmd.clone.sunk | while | flops 1634271232 | bytes 122180872 | solution.py:106
  133.3 9.4 %fusion.65 = f32[4096,128]{1,0:T(8,128)S(1)} fusion(f32[2,512,4096]{2,1,0:T(8,128)} %get-tuple-element.459, s32[]{:T(128)} %get-tuple-element.440, f32[2,512,4096]{2,1,0:T(8,128)} %get-tuple-element.457, f32[512]{0:T(512)S(1)} %bitcast.117, f32[512]{0:T(512)S(1)} %bitcast.114, f32[4096,128]{1,0:T(8,128)S(1)} %get-tuple-element.441, ...), kind=kOutput, calls=%fused_computation.24.clone.1 | convolution fusion | flops 546832384 | bytes 21107712 | tf_op jit(solution)/shard_map/while/body/eval_jaxpr/dot_general | solution.py:30
  142.7 1.2 copy-done
  143.8 5.5 %fusion.66 = bf16[2,512,128]{2,1,0:T(8,128)(2,1)S(1)} fusion(bf16[2,512,128]{2,1,0:T(8,128)(2,1)S(1)} %copy-done.4, s32[]{:T(128)} %get-tuple-element.440, bf16[4096,128]{1,0:T(8,128)(2,1)S(1)} %get-tuple-element.463, f32[2,512,4096]{2,1,0:T(8,128)} %get-tuple-element.459, f32[2,512,4096]{2,1,0:T(8,128)S(1)} %copy-done, f32[512]{0:T(512)S(1)} %bitcast.118, ...), kind=kOutput, calls=%fused_computation.33.clone.1 | convolution fusion | flops 545325056 | bytes 18093056 | tf_op jit(solution)/shard_map/while/body/eval_jaxpr/dot_general | solution.py:99
  150.0 3.6 %convolution_add_fusion.2 = f32[4096,128]{1,0:T(8,128)} fusion(f32[2,512,4096]{2,1,0:T(8,128)S(1)} %copy-done, s32[]{:T(128)} %get-tuple-element.440, f32[512]{0:T(512)S(1)} %bitcast.116, f32[4096,128]{1,0:T(8,128)} %get-tuple-element.442, pred[]{:T(512)S(6)} %compare.3, bf16[2,512,128]{2,1,0:T(8,128)(2,1)S(1)} %copy-done.3), kind=kOutput, calls=%fused_computation.22.clone.1 | convolution fusion | flops 542113792 | bytes 12717057 | tf_op jit(solution)/shard_map/while/body/eval_jaxpr/dot_general | solution.py:30
  153.7 9.4 %fusion.65 = f32[4096,128]{1,0:T(8,128)S(1)} fusion(f32[2,512,4096]{2,1,0:T(8,128)} %get-tuple-element.459, s32[]{:T(128)} %get-tuple-element.440, f32[2,512,4096]{2,1,0:T(8,128)} %get-tuple-element.457, f32[512]{0:T(512)S(1)} %bitcast.117, f32[512]{0:T(512)S(1)} %bitcast.114, f32[4096,128]{1,0:T(8,128)S(1)} %get-tuple-element.441, ...), kind=kOutput, calls=%fused_computation.24.clone.1 | convolution fusion | flops 546832384 | bytes 21107712 | tf_op jit(solution)/shard_map/while/body/eval_jaxpr/dot_general | solution.py:30
  164.2 5.5 %fusion.66 = bf16[2,512,128]{2,1,0:T(8,128)(2,1)S(1)} fusion(bf16[2,512,128]{2,1,0:T(8,128)(2,1)S(1)} %copy-done.4, s32[]{:T(128)} %get-tuple-element.440, bf16[4096,128]{1,0:T(8,128)(2,1)S(1)} %get-tuple-element.463, f32[2,512,4096]{2,1,0:T(8,128)} %get-tuple-element.459, f32[2,512,4096]{2,1,0:T(8,128)S(1)} %copy-done, f32[512]{0:T(512)S(1)} %bitcast.118, ...), kind=kOutput, calls=%fused_computation.33.clone.1 | convolution fusion | flops 545325056 | bytes 18093056 | tf_op jit(solution)/shard_map/while/body/eval_jaxpr/dot_general | solution.py:99
  170.4 5.2 %convolution_add_fusion.2 = f32[4096,128]{1,0:T(8,128)} fusion(f32[2,512,4096]{2,1,0:T(8,128)S(1)} %copy-done, s32[]{:T(128)} %get-tuple-element.440, f32[512]{0:T(512)S(1)} %bitcast.116, f32[4096,128]{1,0:T(8,128)} %get-tuple-element.442, pred[]{:T(512)S(6)} %compare.3, bf16[2,512,128]{2,1,0:T(8,128)(2,1)S(1)} %copy-done.3), kind=kOutput, calls=%fused_computation.22.clone.1 | convolution fusion | flops 542113792 | bytes 12717057 | tf_op jit(solution)/shard_map/while/body/eval_jaxpr/dot_general | solution.py:30
  175.8 1.7 convert.7
  177.5 1.6 pad_maximum_fusion
  179.1 7.1 %reduce-scatter.3.cloned.1.call-done = bf16[512,128]{1,0:T(8,128)(2,1)} async-done(((bf16[1024,128]{1,0:T(8,128)(2,1)}), bf16[512,128]{1,0:T(8,128)(2,1)}) %reduce-scatter.3.cloned.1.call-update) | async-done | bytes 131088 | tf_op jit(solution)/shard_map/reduce_scatter | solution.py:113
  186.2 1.6 convert_element_type.53
  187.8 70.2 %reduce-scatter.5.cloned.1.call-done = bf16[512,256]{1,0:T(8,128)(2,1)} async-done(((bf16[4096,256]{1,0:T(8,128)(2,1)}), bf16[512,256]{1,0:T(8,128)(2,1)}) %reduce-scatter.5.cloned.1.call-update) | async-done | bytes 262160 | tf_op jit(solution)/shard_map/reduce_scatter | solution.py:108
  258.0 1.8 fusion.43
  (60 shorter events, 3.4 us)
Async XLA Ops:
  7.2 46.5 %all-gather.5.cloned.1.call-start = ((), (), s32[]{:S(2)}) async-start(), calls=%async_computation.2 | async-start | bytes 1179648 | tf_op jit(solution)/shard_map/all_gather | solution.py:50
  8.9 86.4 %all-gather.7.cloned.1.call-start = ((), (), s32[]{:S(2)}) async-start(), calls=%async_computation.3 | async-start | bytes 1179648 | tf_op jit(solution)/shard_map/all_gather | solution.py:51
  10.6 175.6 %reduce-scatter.3.cloned.1.call-start = ((), (), s32[]{:S(2)}) async-start(), calls=%async_computation.4 | async-start | bytes 393216 | tf_op jit(solution)/shard_map/reduce_scatter | solution.py:113
  97.7 1.3 copy-start.1
  97.7 1.3 copy-start.2
  108.6 1.4 copy-start.1
  108.6 1.4 copy-start.2
  133.3 10.5 %copy-start = (f32[2,512,4096]{2,1,0:T(8,128)S(1)}, f32[2,512,4096]{2,1,0:T(8,128)}, u32[]{:S(2)}) copy-start(f32[2,512,4096]{2,1,0:T(8,128)} %get-tuple-element.457) | copy-start | bytes 50331652 | tf_op jit(solution)/shard_map/while
  133.3 10.5 %copy-start.4 = (bf16[2,512,128]{2,1,0:T(8,128)(2,1)S(1)}, bf16[2,512,128]{2,1,0:T(8,128)(2,1)}, u32[]{:S(2)}) copy-start(bf16[2,512,128]{2,1,0:T(8,128)(2,1)} %get-tuple-element.443) | copy-start | bytes 786436 | tf_op jit(solution)/shard_map/while
  143.8 6.2 %copy-start.3 = (bf16[2,512,128]{2,1,0:T(8,128)(2,1)S(1)}, bf16[2,512,128]{2,1,0:T(8,128)(2,1)}, u32[]{:S(2)}) copy-start(bf16[2,512,128]{2,1,0:T(8,128)(2,1)} %get-tuple-element.462) | copy-start | bytes 786436 | tf_op jit(solution)/shard_map/while
  149.3 0.7 copy-start.5
  153.6 10.5 %copy-start = (f32[2,512,4096]{2,1,0:T(8,128)S(1)}, f32[2,512,4096]{2,1,0:T(8,128)}, u32[]{:S(2)}) copy-start(f32[2,512,4096]{2,1,0:T(8,128)} %get-tuple-element.457) | copy-start | bytes 50331652 | tf_op jit(solution)/shard_map/while
  153.7 10.5 %copy-start.4 = (bf16[2,512,128]{2,1,0:T(8,128)(2,1)S(1)}, bf16[2,512,128]{2,1,0:T(8,128)(2,1)}, u32[]{:S(2)}) copy-start(bf16[2,512,128]{2,1,0:T(8,128)(2,1)} %get-tuple-element.443) | copy-start | bytes 786436 | tf_op jit(solution)/shard_map/while
  164.2 6.2 %copy-start.3 = (bf16[2,512,128]{2,1,0:T(8,128)(2,1)S(1)}, bf16[2,512,128]{2,1,0:T(8,128)(2,1)}, u32[]{:S(2)}) copy-start(bf16[2,512,128]{2,1,0:T(8,128)(2,1)} %get-tuple-element.462) | copy-start | bytes 786436 | tf_op jit(solution)/shard_map/while
  169.7 0.7 copy-start.5
  175.6 82.4 %reduce-scatter.5.cloned.1.call-start = ((), (), s32[]{:S(2)}) async-start(), calls=%async_computation.5 | async-start | bytes 2359296 | tf_op jit(solution)/shard_map/reduce_scatter | solution.py:108
Sparse Core Ops, SparseCore 0:
  10.7 42.9 all-gather.4
  56.3 38.8 all-gather.6
  175.7 10.4 reduce-scatter.2
  190.0 67.9 reduce-scatter.4
where the time goes:
time: 267 us; the launch traced here: 266 us
  waiting for transfers between devices  145 us (54%)
  matrix products  47.1 us (18%)
  blocking collectives  28.1 us (11%)
  other arithmetic  24.9 us (9%)
  between operations  15.2 us (6%)
  local copies, waits for them, and re-layouts  5.91 us (2%)
    reduce_scatter x1, waiting for transfers between devices, shards(): lax.psum_scatter(stacked.astype(jnp.bfloat16), 'pb', scatter_dimension=0,...  70.2 us
    all_gather x1, waiting for transfers between devices, shards(): lax.all_gather(value_codes.astype(jnp.bfloat16), 'pb', axis=0, tiled=True)  40.2 us
    dot_general x4, matrix products, contract_first(): lax.dot_general(left, right, (((0,), (0,)), ((), ())), preferred_element_...  27.5 us
    all_gather x1, waiting for transfers between devices, shards(): lax.all_gather(key_codes.astype(jnp.bfloat16), 'pb', axis=0, tiled=True)  27.2 us
    dynamic_update_slice x2, other arithmetic, shards(): lax.scan(first_pass, jnp.float32(0.0), (q_blocks, d_blocks))  12.8 us
    dot_general x2, matrix products, second_full(): jnp.dot(d_scores_low, keys, preferred_element_type=jnp.float32) * factor  11 us
    all_gather x2, blocking collectives, merged(): gathered = jax.tree.map(lambda a: lax.all_gather(a, axis), part)  8.68 us
    dot_general x4, matrix products, contract_last(): lax.dot_general(left, right, (((1,), (1,)), ((), ())), preferred_element_...  8.63 us
  transfers between devices with their start and end apart: 4, of which 4 were waited for; matrix products, arithmetic and copies ran while one was open for 3% of the time, Pallas kernels for 0%

commit v1 on v0

--- a/solution.py
+++ b/solution.py
@@ -46,9 +46,26 @@
         lax.all_gather(queries, "ka", axis=0, tiled=True),
         lax.all_gather(out_grad, "ka", axis=0, tiled=True),
     )
+
+    def types_build(vec):
+        along_axis = "pb"
+        num_devices = lax.axis_size(along_axis)
+        series = [(dev, (dev + 1) % num_devices) for dev in range(num_devices)]
+        frames = [(dev, (dev - 1) % num_devices) for dev in range(num_devices)]
+        vec_out, local_out = ([vec], [vec])
+        for _ in range(num_devices // 2):
+            item_now = lax.ppermute(vec_out[-1], perm=series, axis_name=along_axis)
+            vec_out.append(item_now)
+        for _ in range((num_devices - 1) // 2):
+            local_out.append(lax.ppermute(local_out[-1], axis_name=along_axis, perm=frames))
+        piece_out = jnp.concatenate([*vec_out[::-1], *local_out[1:]], axis=0)
+        return jnp.roll(
+            piece_out, (lax.axis_index(along_axis) - num_devices // 2) * vec.shape[0], axis=0
+        )
+
     key_rows, value_rows = (
         lax.all_gather(key_codes.astype(jnp.bfloat16), "pb", axis=0, tiled=True),
-        lax.all_gather(value_codes.astype(jnp.bfloat16), "pb", axis=0, tiled=True),
+        types_build(value_codes.astype(jnp.bfloat16)),
     )
     keys = dequantize(key_rows, key_scale)
     values = dequantize(value_rows, value_scale)

time: 267 us -> 240 us (0.90)
  waiting for transfers between devices: 145 us -> 104 us
  starting transfers between devices: 0.16 us -> 17.4 us
    all_gather x1 -> x0, waiting for transfers between devices: 40.2 us -> none  [shards(): lax.all_gather(value_codes.astype(jnp.bfloat16), 'pb', axis=0, tiled=True)]
    ppermute x0 -> x7, starting transfers between devices: none -> 17.2 us  [the longest x3 14.2 us: types_build(): lax.ppermute(local_out[-1], axis_name=along_axis, perm=frames)]
    all_gather x1, waiting for transfers between devices: 27.2 us -> 14.5 us  [shards(): lax.all_gather(key_codes.astype(jnp.bfloat16), 'pb', axis=0, tiled=True)]
    ppermute x0 -> x7, waiting for transfers between devices: none -> 11.9 us  [the longest x4 9.54 us: types_build(): item_now = lax.ppermute(vec_out[-1], perm=series, axis_name=along_axis)]
  transfers between devices with their start and end apart: 4 -> 10, of which waited for: 4 -> 6; matrix products, arithmetic and copies ran while one was open for 3% -> 3% of each run, Pallas kernels for 0% -> 0%
where the time goes in v1:
time: 240 us; the launch traced here: 239 us
  waiting for transfers between devices  104 us (43%)
  matrix products  47.1 us (20%)
  blocking collectives  26.4 us (11%)
  other arithmetic  23.1 us (10%)
  starting transfers between devices  17.4 us (7%)
  between operations  15.3 us (6%)
  local copies, waits for them, and re-layouts  6.18 us (3%)
    reduce_scatter x1, waiting for transfers between devices, shards(): lax.psum_scatter(stacked.astype(jnp.bfloat16), 'pb', scatter_dimension=0,...  70 us
    dot_general x4, matrix products, contract_first(): lax.dot_general(left, right, (((0,), (0,)), ((), ())), preferred_element_...  27.5 us
    all_gather x1, waiting for transfers between devices, shards(): lax.all_gather(key_codes.astype(jnp.bfloat16), 'pb', axis=0, tiled=True)  14.5 us
    ppermute x3, starting transfers between devices, types_build(): lax.ppermute(local_out[-1], axis_name=along_axis, perm=frames)  14.2 us
    dynamic_update_slice x2, other arithmetic, shards(): lax.scan(first_pass, jnp.float32(0.0), (q_blocks, d_blocks))  12.8 us
    dot_general x2, matrix products, second_full(): jnp.dot(d_scores_low, keys, preferred_element_type=jnp.float32) * factor  11 us
    ppermute x4, waiting for transfers between devices, types_build(): item_now = lax.ppermute(vec_out[-1], perm=series, axis_name=along_axis)  9.54 us
    all_gather x2, blocking collectives, merged(): gathered = jax.tree.map(lambda a: lax.all_gather(a, axis), part)  8.68 us
  transfers between devices with their start and end apart: 10, of which 6 were waited for; matrix products, arithmetic and copies ran while one was open for 3% of the time, Pallas kernels for 0%

profile of v1, /device:TPU:0, one launch (start us, length us, event | category | flops | bytes accessed | tf_op | source)
XLA Modules:
  0.0 239.3 jit_solution(15791258078670510426)
XLA Ops:
  8.2 3.0 %collective-permute-start = (bf16[512,128]{1,0:T(8,128)(2,1)S(1)}, bf16[512,128]{1,0:T(8,128)(2,1)S(1)}, u32[]{:S(2)}, u32[]{:S(2)}) collective-permute-start(bf16[512,128]{1,0:T(8,128)(2,1)S(1)} %convert_element_type.48), channel_id=1, source_target_pairs={{0,4},{4,8},{8,12},{12,16},{16,20},{20,24},{24,28},{28,0},{1,5},{5... | collective-permute-start | bytes 393224 | tf_op jit(solution)/shard_map/ppermute | solution.py:57
  11.2 6.5 %collective-permute-done = bf16[512,128]{1,0:T(8,128)(2,1)S(1)} collective-permute-done((bf16[512,128]{1,0:T(8,128)(2,1)S(1)}, bf16[512,128]{1,0:T(8,128)(2,1)S(1)}, u32[]{:S(2)}, u32[]{:S(2)}) %collective-permute-start) | collective-permute-done | bytes 131104 | tf_op jit(solution)/shard_map/ppermute | solution.py:57
  17.8 4.7 %collective-permute-start.4 = (bf16[512,128]{1,0:T(8,128)(2,1)S(1)}, bf16[512,128]{1,0:T(8,128)(2,1)S(1)}, u32[]{:S(2)}, u32[]{:S(2)}) collective-permute-start(bf16[512,128]{1,0:T(8,128)(2,1)S(1)} %convert_element_type.48), channel_id=1, source_target_pairs={{0,28},{4,0},{8,4},{12,8},{16,12},{20,16},{24,20},{28,24},{1,29},{... | collective-permute-start | bytes 393224 | tf_op jit(solution)/shard_map/ppermute | solution.py:60
  22.5 3.0 %collective-permute-done.1 = bf16[512,128]{1,0:T(8,128)(2,1)S(1)} collective-permute-done((bf16[512,128]{1,0:T(8,128)(2,1)S(1)}, bf16[512,128]{1,0:T(8,128)(2,1)S(1)}, u32[]{:S(2)}, u32[]{:S(2)}) %collective-permute-start.1) | collective-permute-done | bytes 131104 | tf_op jit(solution)/shard_map/ppermute | solution.py:57
  25.6 1.6 convert_element_type.45
  28.7 4.7 %collective-permute-start.5 = (bf16[512,128]{1,0:T(8,128)(2,1)S(1)}, bf16[512,128]{1,0:T(8,128)(2,1)S(1)}, u32[]{:S(2)}, u32[]{:S(2)}) collective-permute-start(bf16[512,128]{1,0:T(8,128)(2,1)S(1)} %collective-permute-done.4), channel_id=1, source_target_pairs={{0,28},{4,0},{8,4},{12,8},{16,12},{20,16},{24,20},{28,24},{1,29},{... | collective-permute-start | bytes 393224 | tf_op jit(solution)/shard_map/ppermute | solution.py:60
  33.4 5.8 %all_gather.15 = bf16[1024,128]{1,0:T(8,128)(2,1)S(1)} all-gather(bf16[512,128]{1,0:T(8,128)(2,1)} %param.10), channel_id=1, replica_groups=mesh['pb'=8,'ka'=2,'ha'=2] {'ka'}, dimensions={0}, use_global_device_ids=true | all-gather | bytes 393216 | tf_op jit(solution)/shard_map/all_gather | solution.py:46
  39.2 7.0 %all_gather.17 = bf16[1024,128]{1,0:T(8,128)(2,1)} all-gather(bf16[512,128]{1,0:T(8,128)(2,1)} %param.15), channel_id=1, replica_groups=mesh['pb'=8,'ka'=2,'ha'=2] {'ka'}, dimensions={0}, use_global_device_ids=true | all-gather | bytes 393216 | tf_op jit(solution)/shard_map/all_gather | solution.py:47
  46.2 4.7 %collective-permute-start.6 = (bf16[512,128]{1,0:T(8,128)(2,1)S(1)}, bf16[512,128]{1,0:T(8,128)(2,1)S(1)}, u32[]{:S(2)}, u32[]{:S(2)}) collective-permute-start(bf16[512,128]{1,0:T(8,128)(2,1)S(1)} %collective-permute-done.5), channel_id=1, source_target_pairs={{0,28},{4,0},{8,4},{12,8},{16,12},{20,16},{24,20},{28,24},{1,29},{... | collective-permute-start | bytes 393224 | tf_op jit(solution)/shard_map/ppermute | solution.py:60
  51.1 2.3 collective-permute-done.6
  54.9 14.5 %all-gather.4.cloned.1.call-done = bf16[4096,128]{1,0:T(8,128)(2,1)} async-done(((bf16[512,128]{1,0:T(8,128)(2,1)}), bf16[4096,128]{1,0:T(8,128)(2,1)}) %all-gather.4.cloned.1.call-update) | async-done | bytes 1048592 | tf_op jit(solution)/shard_map/all_gather | solution.py:67
  70.8 21.8 %while.13 = (s32[]{:T(128)}, f32[2,512]{1,0:T(2,128)S(1)}, f32[2,512]{1,0:T(2,128)S(1)}, f32[2,512]{1,0:T(2,128)S(1)}, f32[2,512,4096]{2,1,0:T(8,128)}, /*index=...) while((s32[]{:T(128)}, f32[2,512]{1,0:T(2,128)S(1)}, ...), condition=%wide.region_4.5_spmd, body=%wide.region_0.4_spmd.sunk | while | flops 1090517504 | bytes 66343616 | solution.py:95
  72.2 3.0 %multiply_reduce_fusion.5 = (f32[512]{0:T(512)S(1)}, f32[512]{0:T(512)S(1)}, f32[512,4096]{1,0:T(8,128)S(1)}) fusion(f32[512,4096]{1,0:T(8,128)S(1)} %get-tuple-element.372, f32[512]{0:T(512)S(1)} %get-tuple-element.371, bf16[4096,128]{1,0:T(8,128)(2,1)S(1)} %copy-done.1, bf16[2,512,128]{2,1,0:T(8,128)(2,1)S(1)} %copy-done.2, s32[]{:T(128)} %get-tuple-element.403), kind=kOutput, calls=%fused_computation.2.clone.1 | convolution fusion | flops 547355648 | bytes 17963012 | tf_op jit(solution)/shard_map/while/body/eval_jaxpr/dot_general | solution.py:24
  75.2 6.4 %bitcast_dynamic-update-slice_fusion.3 = (f32[2,512,4096]{2,1,0:T(8,128)}, f32[2,512,4096]{2,1,0:T(8,128)}) fusion(f32[2,512,4096]{2,1,0:T(8,128)} %get-tuple-element.408, s32[]{:T(128)} %get-tuple-element.403, f32[512,4096]{1,0:T(8,128)S(1)} %get-tuple-element.375, f32[2,512,4096]{2,1,0:T(8,128)} %get-tuple-element.407, ...), kind=kLoop, calls=%fused_computation.clone.1 | loop fusion | flops 2097152 | bytes 33554944 | tf_op jit(solution)/shard_map/while/body/jit(dynamic_update_index_in_dim)/dynamic_update_slice | solution.py:95
  83.1 3.0 %multiply_reduce_fusion.5 = (f32[512]{0:T(512)S(1)}, f32[512]{0:T(512)S(1)}, f32[512,4096]{1,0:T(8,128)S(1)}) fusion(f32[512,4096]{1,0:T(8,128)S(1)} %get-tuple-element.372, f32[512]{0:T(512)S(1)} %get-tuple-element.371, bf16[4096,128]{1,0:T(8,128)(2,1)S(1)} %copy-done.1, bf16[2,512,128]{2,1,0:T(8,128)(2,1)S(1)} %copy-done.2, s32[]{:T(128)} %get-tuple-element.403), kind=kOutput, calls=%fused_computation.2.clone.1 | convolution fusion | flops 547355648 | bytes 17963012 | tf_op jit(solution)/shard_map/while/body/eval_jaxpr/dot_general | solution.py:24
  86.1 6.4 %bitcast_dynamic-update-slice_fusion.3 = (f32[2,512,4096]{2,1,0:T(8,128)}, f32[2,512,4096]{2,1,0:T(8,128)}) fusion(f32[2,512,4096]{2,1,0:T(8,128)} %get-tuple-element.408, s32[]{:T(128)} %get-tuple-element.403, f32[512,4096]{1,0:T(8,128)S(1)} %get-tuple-element.375, f32[2,512,4096]{2,1,0:T(8,128)} %get-tuple-element.407, ...), kind=kLoop, calls=%fused_computation.clone.1 | loop fusion | flops 2097152 | bytes 33554944 | tf_op jit(solution)/shard_map/while/body/jit(dynamic_update_index_in_dim)/dynamic_update_slice | solution.py:95
  92.6 4.3 %all-gather = f32[2,1,1024]{2,1,0:T(1,128)S(1)} all-gather(f32[1,1,1024]{2,1,0:T(1,128)S(1)} %reshape.58), channel_id=1, replica_groups=mesh['pb'=8,'ka'=2,'ha'=2] {'ka'}, dimensions={0}, use_global_device_ids=true | all-gather | bytes 12288 | tf_op jit(solution)/shard_map/all_gather | solution.py:9
  97.0 4.3 %all-gather.1 = f32[2,1,1024]{2,1,0:T(1,128)S(1)} all-gather(f32[1,1,1024]{2,1,0:T(1,128)S(1)} %reshape.60), channel_id=1, replica_groups=mesh['pb'=8,'ka'=2,'ha'=2] {'ka'}, dimensions={0}, use_global_device_ids=true | all-gather | bytes 12288 | tf_op jit(solution)/shard_map/all_gather | solution.py:9
  101.4 4.9 %psum.7 = f32[2,512]{1,0:T(2,128)S(1)} all-reduce(f32[2,512]{1,0:T(2,128)S(1)} %reshape.57), channel_id=1, replica_groups=mesh['pb'=8,'ka'=2,'ha'=2] {'ka'}, use_global_device_ids=true, to_apply=%region_5.6 | all-reduce | flops 1024 | bytes 8192 | tf_op jit(solution)/shard_map/psum | solution.py:103
  106.4 42.3 %while.40 = (s32[]{:T(128)}, f32[4096,128]{1,0:T(8,128)S(1)}, f32[4096,128]{1,0:T(8,128)}, bf16[2,512,128]{2,1,0:T(8,128)(2,1)}, f32[2,512,4096]{2,1,0:T(8,128)}...) while((s32[]{:T(128)}, f32[4096,128]{1,0:T(8,128)S(1)}, ...), condition=%wide.region_7.8_spmd.clone, body=%wide.region_6.7_spmd.clone.sunk | while | flops 1634271232 | bytes 122180872 | solution.py:123
  106.5 9.4 %fusion.65 = f32[4096,128]{1,0:T(8,128)S(1)} fusion(f32[2,512,4096]{2,1,0:T(8,128)} %get-tuple-element.459, s32[]{:T(128)} %get-tuple-element.440, f32[2,512,4096]{2,1,0:T(8,128)} %get-tuple-element.457, f32[512]{0:T(512)S(1)} %bitcast.117, f32[512]{0:T(512)S(1)} %bitcast.114, f32[4096,128]{1,0:T(8,128)S(1)} %get-tuple-element.441, ...), kind=kOutput, calls=%fused_computation.24.clone.1 | convolution fusion | flops 546832384 | bytes 21107712 | tf_op jit(solution)/shard_map/while/body/eval_jaxpr/dot_general | solution.py:30
  117.0 5.5 %fusion.66 = bf16[2,512,128]{2,1,0:T(8,128)(2,1)S(1)} fusion(bf16[2,512,128]{2,1,0:T(8,128)(2,1)S(1)} %copy-done.5, s32[]{:T(128)} %get-tuple-element.440, bf16[4096,128]{1,0:T(8,128)(2,1)S(1)} %get-tuple-element.463, f32[2,512,4096]{2,1,0:T(8,128)} %get-tuple-element.459, f32[2,512,4096]{2,1,0:T(8,128)S(1)} %copy-done, f32[512]{0:T(512)S(1)} %bitcast.118, ...), kind=kOutput, calls=%fused_computation.33.clone.1 | convolution fusion | flops 545325056 | bytes 18093056 | tf_op jit(solution)/shard_map/while/body/eval_jaxpr/dot_general | solution.py:116
  123.2 3.6 %convolution_add_fusion.2 = f32[4096,128]{1,0:T(8,128)} fusion(f32[2,512,4096]{2,1,0:T(8,128)S(1)} %copy-done, s32[]{:T(128)} %get-tuple-element.440, f32[512]{0:T(512)S(1)} %bitcast.116, f32[4096,128]{1,0:T(8,128)} %get-tuple-element.442, pred[]{:T(512)S(6)} %compare.4, bf16[2,512,128]{2,1,0:T(8,128)(2,1)S(1)} %copy-done.3), kind=kOutput, calls=%fused_computation.22.clone.1 | convolution fusion | flops 542113792 | bytes 12717057 | tf_op jit(solution)/shard_map/while/body/eval_jaxpr/dot_general | solution.py:30
  126.8 9.4 %fusion.65 = f32[4096,128]{1,0:T(8,128)S(1)} fusion(f32[2,512,4096]{2,1,0:T(8,128)} %get-tuple-element.459, s32[]{:T(128)} %get-tuple-element.440, f32[2,512,4096]{2,1,0:T(8,128)} %get-tuple-element.457, f32[512]{0:T(512)S(1)} %bitcast.117, f32[512]{0:T(512)S(1)} %bitcast.114, f32[4096,128]{1,0:T(8,128)S(1)} %get-tuple-element.441, ...), kind=kOutput, calls=%fused_computation.24.clone.1 | convolution fusion | flops 546832384 | bytes 21107712 | tf_op jit(solution)/shard_map/while/body/eval_jaxpr/dot_general | solution.py:30
  137.3 5.5 %fusion.66 = bf16[2,512,128]{2,1,0:T(8,128)(2,1)S(1)} fusion(bf16[2,512,128]{2,1,0:T(8,128)(2,1)S(1)} %copy-done.5, s32[]{:T(128)} %get-tuple-element.440, bf16[4096,128]{1,0:T(8,128)(2,1)S(1)} %get-tuple-element.463, f32[2,512,4096]{2,1,0:T(8,128)} %get-tuple-element.459, f32[2,512,4096]{2,1,0:T(8,128)S(1)} %copy-done, f32[512]{0:T(512)S(1)} %bitcast.118, ...), kind=kOutput, calls=%fused_computation.33.clone.1 | convolution fusion | flops 545325056 | bytes 18093056 | tf_op jit(solution)/shard_map/while/body/eval_jaxpr/dot_general | solution.py:116
  143.5 5.2 %convolution_add_fusion.2 = f32[4096,128]{1,0:T(8,128)} fusion(f32[2,512,4096]{2,1,0:T(8,128)S(1)} %copy-done, s32[]{:T(128)} %get-tuple-element.440, f32[512]{0:T(512)S(1)} %bitcast.116, f32[4096,128]{1,0:T(8,128)} %get-tuple-element.442, pred[]{:T(512)S(6)} %compare.4, bf16[2,512,128]{2,1,0:T(8,128)(2,1)S(1)} %copy-done.3), kind=kOutput, calls=%fused_computation.22.clone.1 | convolution fusion | flops 542113792 | bytes 12717057 | tf_op jit(solution)/shard_map/while/body/eval_jaxpr/dot_general | solution.py:30
  148.9 1.7 convert.7
  150.6 1.6 pad_maximum_fusion
  152.2 7.1 %reduce-scatter.3.cloned.1.call-done = bf16[512,128]{1,0:T(8,128)(2,1)} async-done(((bf16[1024,128]{1,0:T(8,128)(2,1)}), bf16[512,128]{1,0:T(8,128)(2,1)}) %reduce-scatter.3.cloned.1.call-update) | async-done | bytes 131088 | tf_op jit(solution)/shard_map/reduce_scatter | solution.py:130
  159.3 1.6 convert_element_type.53
  160.9 70.0 %reduce-scatter.5.cloned.1.call-done = bf16[512,256]{1,0:T(8,128)(2,1)} async-done(((bf16[4096,256]{1,0:T(8,128)(2,1)}), bf16[512,256]{1,0:T(8,128)(2,1)}) %reduce-scatter.5.cloned.1.call-update) | async-done | bytes 262160 | tf_op jit(solution)/shard_map/reduce_scatter | solution.py:125
  231.0 1.8 fusion.43
  (89 shorter events, 11.2 us)
Async XLA Ops:
  7.2 43.8 %copy-start.4 = (s32[512,128]{1,0:T(8,128)S(1)}, s32[512,128]{1,0:T(8,128)}, u32[]{:S(2)}) copy-start(s32[512,128]{1,0:T(8,128)} %param.12) | copy-start | bytes 786436
  7.2 62.2 %all-gather.4.cloned.1.call-start = ((), (), s32[]{:S(2)}) async-start(), calls=%async_computation.2 | async-start | bytes 1179648 | tf_op jit(solution)/shard_map/all_gather | solution.py:67
  8.2 9.6 %collective-permute-start = (bf16[512,128]{1,0:T(8,128)(2,1)S(1)}, bf16[512,128]{1,0:T(8,128)(2,1)S(1)}, u32[]{:S(2)}, u32[]{:S(2)}) collective-permute-start(bf16[512,128]{1,0:T(8,128)(2,1)S(1)} %convert_element_type.48), channel_id=1, source_target_pairs={{0,4},{4,8},{8,12},{12,16},{16,20},{20,24},{24,28},{28,0},{1,5},{5... | collective-permute-start | bytes 393224 | tf_op jit(solution)/shard_map/ppermute | solution.py:57
  17.8 7.7 %collective-permute-start.1 = (bf16[512,128]{1,0:T(8,128)(2,1)S(1)}, bf16[512,128]{1,0:T(8,128)(2,1)S(1)}, u32[]{:S(2)}, u32[]{:S(2)}) collective-permute-start(bf16[512,128]{1,0:T(8,128)(2,1)S(1)} %collective-permute-done), channel_id=1, source_target_pairs={{0,4},{4,8},{8,12},{12,16},{16,20},{20,24},{24,28},{28,0},{1,5},{5... | collective-permute-start | bytes 393224 | tf_op jit(solution)/shard_map/ppermute | solution.py:57
  17.8 10.9 %collective-permute-start.4 = (bf16[512,128]{1,0:T(8,128)(2,1)S(1)}, bf16[512,128]{1,0:T(8,128)(2,1)S(1)}, u32[]{:S(2)}, u32[]{:S(2)}) collective-permute-start(bf16[512,128]{1,0:T(8,128)(2,1)S(1)} %convert_element_type.48), channel_id=1, source_target_pairs={{0,28},{4,0},{8,4},{12,8},{16,12},{20,16},{24,20},{28,24},{1,29},{... | collective-permute-start | bytes 393224 | tf_op jit(solution)/shard_map/ppermute | solution.py:60
  25.5 7.9 %collective-permute-start.2 = (bf16[512,128]{1,0:T(8,128)(2,1)S(1)}, bf16[512,128]{1,0:T(8,128)(2,1)S(1)}, u32[]{:S(2)}, u32[]{:S(2)}) collective-permute-start(bf16[512,128]{1,0:T(8,128)(2,1)S(1)} %collective-permute-done.1), channel_id=1, source_target_pairs={{0,4},{4,8},{8,12},{12,16},{16,20},{20,24},{24,28},{28,0},{1,5},{5... | collective-permute-start | bytes 393224 | tf_op jit(solution)/shard_map/ppermute | solution.py:57
  27.2 132.1 %reduce-scatter.3.cloned.1.call-start = ((), (), s32[]{:S(2)}) async-start(), calls=%async_computation.3 | async-start | bytes 393216 | tf_op jit(solution)/shard_map/reduce_scatter | solution.py:130
  28.7 17.5 %collective-permute-start.5 = (bf16[512,128]{1,0:T(8,128)(2,1)S(1)}, bf16[512,128]{1,0:T(8,128)(2,1)S(1)}, u32[]{:S(2)}, u32[]{:S(2)}) collective-permute-start(bf16[512,128]{1,0:T(8,128)(2,1)S(1)} %collective-permute-done.4), channel_id=1, source_target_pairs={{0,28},{4,0},{8,4},{12,8},{16,12},{20,16},{24,20},{28,24},{1,29},{... | collective-permute-start | bytes 393224 | tf_op jit(solution)/shard_map/ppermute | solution.py:60
  33.4 17.5 %collective-permute-start.3 = (bf16[512,128]{1,0:T(8,128)(2,1)S(1)}, bf16[512,128]{1,0:T(8,128)(2,1)S(1)}, u32[]{:S(2)}, u32[]{:S(2)}) collective-permute-start(bf16[512,128]{1,0:T(8,128)(2,1)S(1)} %collective-permute-done.2), channel_id=1, source_target_pairs={{0,4},{4,8},{8,12},{12,16},{16,20},{20,24},{24,28},{28,0},{1,5},{5... | collective-permute-start | bytes 393224 | tf_op jit(solution)/shard_map/ppermute | solution.py:57
  46.2 7.2 %collective-permute-start.6 = (bf16[512,128]{1,0:T(8,128)(2,1)S(1)}, bf16[512,128]{1,0:T(8,128)(2,1)S(1)}, u32[]{:S(2)}, u32[]{:S(2)}) collective-permute-start(bf16[512,128]{1,0:T(8,128)(2,1)S(1)} %collective-permute-done.5), channel_id=1, source_target_pairs={{0,28},{4,0},{8,4},{12,8},{16,12},{20,16},{24,20},{28,24},{1,29},{... | collective-permute-start | bytes 393224 | tf_op jit(solution)/shard_map/ppermute | solution.py:60
  70.8 1.4 copy-start.1
  70.8 1.4 copy-start.2
  81.7 1.4 copy-start.1
  81.7 1.4 copy-start.2
  106.4 10.5 %copy-start = (f32[2,512,4096]{2,1,0:T(8,128)S(1)}, f32[2,512,4096]{2,1,0:T(8,128)}, u32[]{:S(2)}) copy-start(f32[2,512,4096]{2,1,0:T(8,128)} %get-tuple-element.457) | copy-start | bytes 50331652 | tf_op jit(solution)/shard_map/while
  106.4 10.5 %copy-start.5 = (bf16[2,512,128]{2,1,0:T(8,128)(2,1)S(1)}, bf16[2,512,128]{2,1,0:T(8,128)(2,1)}, u32[]{:S(2)}) copy-start(bf16[2,512,128]{2,1,0:T(8,128)(2,1)} %get-tuple-element.443) | copy-start | bytes 786436 | tf_op jit(solution)/shard_map/while
  117.0 6.2 %copy-start.3 = (bf16[2,512,128]{2,1,0:T(8,128)(2,1)S(1)}, bf16[2,512,128]{2,1,0:T(8,128)(2,1)}, u32[]{:S(2)}) copy-start(bf16[2,512,128]{2,1,0:T(8,128)(2,1)} %get-tuple-element.462) | copy-start | bytes 786436 | tf_op jit(solution)/shard_map/while
  122.5 0.7 copy-start.6
  126.8 10.5 %copy-start = (f32[2,512,4096]{2,1,0:T(8,128)S(1)}, f32[2,512,4096]{2,1,0:T(8,128)}, u32[]{:S(2)}) copy-start(f32[2,512,4096]{2,1,0:T(8,128)} %get-tuple-element.457) | copy-start | bytes 50331652 | tf_op jit(solution)/shard_map/while
  126.8 10.5 %copy-start.5 = (bf16[2,512,128]{2,1,0:T(8,128)(2,1)S(1)}, bf16[2,512,128]{2,1,0:T(8,128)(2,1)}, u32[]{:S(2)}) copy-start(bf16[2,512,128]{2,1,0:T(8,128)(2,1)} %get-tuple-element.443) | copy-start | bytes 786436 | tf_op jit(solution)/shard_map/while
  137.3 6.2 %copy-start.3 = (bf16[2,512,128]{2,1,0:T(8,128)(2,1)S(1)}, bf16[2,512,128]{2,1,0:T(8,128)(2,1)}, u32[]{:S(2)}) copy-start(bf16[2,512,128]{2,1,0:T(8,128)(2,1)} %get-tuple-element.462) | copy-start | bytes 786436 | tf_op jit(solution)/shard_map/while
  142.8 0.7 copy-start.6
  148.7 82.2 %reduce-scatter.5.cloned.1.call-start = ((), (), s32[]{:S(2)}) async-start(), calls=%async_computation.4 | async-start | bytes 2359296 | tf_op jit(solution)/shard_map/reduce_scatter | solution.py:125
Sparse Core Ops, SparseCore 0:
  27.3 42.0 all-gather.3
  148.8 10.4 reduce-scatter.2
  163.3 67.6 reduce-scatter.4
